TPU v7x, 512 devices: a whole 4x4x16 slice. The times are simulated.
512 devices in a mesh: space: 32 (over y, x, core), blk: 16 (over z).
Axes of the slice: x: 4, y: 4, z: 16, core: 2. Of those that a mesh axis runs over, the one named last changes fastest.
Arguments:
- snapshots: bfloat16 [20480, 16384], P('blk', 'space'), may hold values from -6 to 6
- row_scales: float32 [20480], P('blk'), may hold values from 0.3 to 3
- block_offsets: int32 [64], P('blk'), may hold values from 0 to 768, as said below
- freq_index: int32 [16], replicated, may hold values from 1 to 255
Outputs:
- modes: float32 [16, 16384, 128], P('blk', 'space')
- r_factor: float32 [16, 2, 64, 64], P('blk')
Inputs may be any that keep to these rules, and one draw needn't show every extreme that they name: `block_offsets`: block offsets index the snapshots held by the block's own index of blk; within every group of 4 blocks they are distinct and increasing, block i of a group lies between i * 256 - 512 / 4 and i * 256 + 512 / 4; in the first group the first is 0 and the last is 768.
All inputs are finite; a program needn't handle non-finite values.
Results may differ from a plain program's by a relative error of at most 0.0064.
Values may be sent and summed in bfloat16 or wider, within the bound.
A program may use at most 64 MiB of HBM per device.

v0:
```python
import math

import jax
import jax.numpy as jnp
from jax import lax
from jax.sharding import PartitionSpec as P

NFFT = 512


def merged(value, axis, combine):
    everything = lax.all_gather(value, axis)
    initial = everything[0]

    def lap(k, so_far):
        return combine(so_far, everything[k])

    return lax.fori_loop(1, lax.axis_size(axis), lap, initial)


def trig_table(freq_index):
    times = jnp.arange(NFFT, dtype=jnp.int32)
    phase = freq_index[:, None] * times[None, :] % NFFT
    angle = 2.0 * math.pi / NFFT * phase.astype(jnp.float32)
    inv_root = 1.0 / math.sqrt(NFFT)
    table = (
        jnp.stack([jnp.cos(angle), -jnp.sin(angle)], 1).reshape(2 * freq_index.shape[0], NFFT)
        * inv_root
    )
    hann = 0.5 - 0.5 * jnp.cos(2.0 * math.pi / NFFT * times.astype(jnp.float32))
    return (table, hann)


def upper_of(matrix):
    return jnp.swapaxes(jnp.linalg.cholesky(matrix), -1, -2)


def merge_pair(first_r, second_r):
    summed = jnp.einsum("fka,fkb->fab", first_r, first_r, precision=lax.Precision.HIGHEST)
    summed = summed + jnp.einsum(
        "fka,fkb->fab", second_r, second_r, precision=lax.Precision.HIGHEST
    )
    return upper_of(summed)


def stacked_gram(regrouped, total_points):
    pairs = regrouped.reshape(regrouped.shape[0], regrouped.shape[1], -1, 2)
    rotated = jnp.stack([-pairs[..., 1], pairs[..., 0]], -1).reshape(regrouped.shape)
    stacked = jnp.concatenate([regrouped, rotated], 1)
    return (
        jnp.einsum("fpa,fpb->fab", stacked, stacked, preferred_element_type=jnp.float32)
        / total_points
    )


def local(snapshots, row_scales, block_offsets, freq_index):
    table, hann = trig_table(freq_index)
    blocks_here = block_offsets.shape[0]
    points_here = snapshots.shape[1]
    freq_count = freq_index.shape[0]
    windows = jax.vmap(lambda start: lax.dynamic_slice_in_dim(snapshots, start, NFFT, 0))(
        block_offsets
    )
    scaled = jax.vmap(lambda start: lax.dynamic_slice_in_dim(row_scales, start, NFFT, 0))(
        block_offsets
    )
    coeffs = (table[None, :, :] * (hann[None, :] * scaled)[:, None, :]).astype(jnp.bfloat16)
    spectra = jnp.einsum(
        "bkt,btp->bkp", coeffs, windows, preferred_element_type=jnp.float32
    ).astype(jnp.bfloat16)
    spectra = spectra.reshape(blocks_here, freq_count, 2, points_here).transpose(1, 3, 0, 2)
    spectra = spectra.reshape(freq_count, points_here, 2 * blocks_here)
    regrouped = lax.all_to_all(spectra, "blk", split_axis=0, concat_axis=2, tiled=True)
    total_points = points_here * lax.axis_size("space")
    upper = merged(upper_of(stacked_gram(regrouped, total_points)), "space", merge_pair)
    lower_factor = jnp.swapaxes(upper, 1, 2)
    width = lower_factor.shape[-1]
    identity = jnp.broadcast_to(jnp.eye(width, dtype=jnp.float32), lower_factor.shape)
    inverse_lower = jax.scipy.linalg.solve_triangular(lower_factor, identity, lower=True)
    modes = jnp.einsum(
        "fpa,fba->fpb",
        regrouped.astype(jnp.float32),
        inverse_lower,
        precision=lax.Precision.HIGHEST,
    )
    r_factor = jnp.stack([upper[:, 0::2, 0::2], upper[:, 0::2, 1::2]], 1)
    return (modes, r_factor)


def solution(mesh):
    return jax.shard_map(
        local,
        mesh=mesh,
        in_specs=(P("blk", "space"), P("blk"), P("blk"), P()),
        out_specs=(P("blk", "space", None), P("blk", None, None, None)),
        check_vma=False,
    )
```

profile of v0, /device:TPU:1, one launch (start us, length us, event | category | flops | bytes accessed | tf_op | source)
XLA Modules:
  0.0 601.2 jit_solution(12262254772496372150)
XLA Ops:
  27.4 27.5 %all_to_all.18 = bf16[16,512,8]{1,2,0:T(8,128)(2,1)S(1)} all-to-all(bf16[16,512,8]{1,2,0:T(8,128)(2,1)S(1)} %copy.55), channel_id=1, replica_groups=mesh['space'=32,'blk'=16] {'blk'}, dimensions={0} | all-to-all | bytes 262144 | tf_op jit(solution)/shard_map/all_to_all | solution.py:73
  56.0 11.7 %custom-call.10 = f32[1,128,128]{2,1,0:T(8,128)S(1)} custom-call(f32[1,128,128]{2,1,0:T(8,128)S(1)} %fusion.11), custom_call_target="Cholesky" | custom-call | tf_op jit(solution)/shard_map/jit(cholesky)/cholesky | solution.py:35
  69.8 55.5 %all-gather.3.cloned.1.call-done = f32[32,128,128]{2,1,0:T(8,128)} async-done(((f32[1,128,128]{2,1,0:T(8,128)}), f32[32,128,128]{2,1,0:T(8,128)}) %all-gather.3.cloned.1.call-update) | async-done | bytes 2097168 | tf_op jit(solution)/shard_map/all_gather | solution.py:12
  126.3 455.0 %while.17 = (s32[]{:T(128)}, f32[1,128,128]{1,2,0:T(8,128)S(1)}, f32[32,1,128,128]{3,2,1,0:T(8,128)}, s32[]{:T(128)}, s32[]{:T(128)}, /*index=5*/s32[]{:T(128)}) while((s32[]{:T(128)}, f32[1,128,128]{1,2,0:T(8,128)S(1)}, f32[32,1,128,128]{3,2,1,0:T(8,128)}, s32[]{:T(128)}, s32[]{:T(128)}, /*index=5*/s32[]{:T(128)}) %tuple.81), condition=%wide.region_3.5_spmd, body=%wide.region_2.4_spmd.sunk | while | flops 50479232 | bytes 853109 | solution.py:18
  127.9 11.7 %custom-call.14 = f32[1,128,128]{2,1,0:T(8,128)S(1)} custom-call(f32[1,128,128]{2,1,0:T(8,128)S(1)} %fusion.32), custom_call_target="Cholesky" | custom-call | tf_op jit(solution)/shard_map/while/body/eval_jaxpr/jit(cholesky)/cholesky | solution.py:35
  142.6 11.7 %custom-call.14 = f32[1,128,128]{2,1,0:T(8,128)S(1)} custom-call(f32[1,128,128]{2,1,0:T(8,128)S(1)} %fusion.32), custom_call_target="Cholesky" | custom-call | tf_op jit(solution)/shard_map/while/body/eval_jaxpr/jit(cholesky)/cholesky | solution.py:35
  157.2 11.7 %custom-call.14 = f32[1,128,128]{2,1,0:T(8,128)S(1)} custom-call(f32[1,128,128]{2,1,0:T(8,128)S(1)} %fusion.32), custom_call_target="Cholesky" | custom-call | tf_op jit(solution)/shard_map/while/body/eval_jaxpr/jit(cholesky)/cholesky | solution.py:35
  171.9 11.7 %custom-call.14 = f32[1,128,128]{2,1,0:T(8,128)S(1)} custom-call(f32[1,128,128]{2,1,0:T(8,128)S(1)} %fusion.32), custom_call_target="Cholesky" | custom-call | tf_op jit(solution)/shard_map/while/body/eval_jaxpr/jit(cholesky)/cholesky | solution.py:35
  186.6 11.7 %custom-call.14 = f32[1,128,128]{2,1,0:T(8,128)S(1)} custom-call(f32[1,128,128]{2,1,0:T(8,128)S(1)} %fusion.32), custom_call_target="Cholesky" | custom-call | tf_op jit(solution)/shard_map/while/body/eval_jaxpr/jit(cholesky)/cholesky | solution.py:35
  201.3 11.7 %custom-call.14 = f32[1,128,128]{2,1,0:T(8,128)S(1)} custom-call(f32[1,128,128]{2,1,0:T(8,128)S(1)} %fusion.32), custom_call_target="Cholesky" | custom-call | tf_op jit(solution)/shard_map/while/body/eval_jaxpr/jit(cholesky)/cholesky | solution.py:35
  215.9 11.7 %custom-call.14 = f32[1,128,128]{2,1,0:T(8,128)S(1)} custom-call(f32[1,128,128]{2,1,0:T(8,128)S(1)} %fusion.32), custom_call_target="Cholesky" | custom-call | tf_op jit(solution)/shard_map/while/body/eval_jaxpr/jit(cholesky)/cholesky | solution.py:35
  230.6 11.7 %custom-call.14 = f32[1,128,128]{2,1,0:T(8,128)S(1)} custom-call(f32[1,128,128]{2,1,0:T(8,128)S(1)} %fusion.32), custom_call_target="Cholesky" | custom-call | tf_op jit(solution)/shard_map/while/body/eval_jaxpr/jit(cholesky)/cholesky | solution.py:35
  245.3 11.7 %custom-call.14 = f32[1,128,128]{2,1,0:T(8,128)S(1)} custom-call(f32[1,128,128]{2,1,0:T(8,128)S(1)} %fusion.32), custom_call_target="Cholesky" | custom-call | tf_op jit(solution)/shard_map/while/body/eval_jaxpr/jit(cholesky)/cholesky | solution.py:35
  259.9 11.7 %custom-call.14 = f32[1,128,128]{2,1,0:T(8,128)S(1)} custom-call(f32[1,128,128]{2,1,0:T(8,128)S(1)} %fusion.32), custom_call_target="Cholesky" | custom-call | tf_op jit(solution)/shard_map/while/body/eval_jaxpr/jit(cholesky)/cholesky | solution.py:35
  274.6 11.7 %custom-call.14 = f32[1,128,128]{2,1,0:T(8,128)S(1)} custom-call(f32[1,128,128]{2,1,0:T(8,128)S(1)} %fusion.32), custom_call_target="Cholesky" | custom-call | tf_op jit(solution)/shard_map/while/body/eval_jaxpr/jit(cholesky)/cholesky | solution.py:35
  289.3 11.7 %custom-call.14 = f32[1,128,128]{2,1,0:T(8,128)S(1)} custom-call(f32[1,128,128]{2,1,0:T(8,128)S(1)} %fusion.32), custom_call_target="Cholesky" | custom-call | tf_op jit(solution)/shard_map/while/body/eval_jaxpr/jit(cholesky)/cholesky | solution.py:35
  304.0 11.7 %custom-call.14 = f32[1,128,128]{2,1,0:T(8,128)S(1)} custom-call(f32[1,128,128]{2,1,0:T(8,128)S(1)} %fusion.32), custom_call_target="Cholesky" | custom-call | tf_op jit(solution)/shard_map/while/body/eval_jaxpr/jit(cholesky)/cholesky | solution.py:35
  318.6 11.7 %custom-call.14 = f32[1,128,128]{2,1,0:T(8,128)S(1)} custom-call(f32[1,128,128]{2,1,0:T(8,128)S(1)} %fusion.32), custom_call_target="Cholesky" | custom-call | tf_op jit(solution)/shard_map/while/body/eval_jaxpr/jit(cholesky)/cholesky | solution.py:35
  333.3 11.7 %custom-call.14 = f32[1,128,128]{2,1,0:T(8,128)S(1)} custom-call(f32[1,128,128]{2,1,0:T(8,128)S(1)} %fusion.32), custom_call_target="Cholesky" | custom-call | tf_op jit(solution)/shard_map/while/body/eval_jaxpr/jit(cholesky)/cholesky | solution.py:35
  348.0 11.7 %custom-call.14 = f32[1,128,128]{2,1,0:T(8,128)S(1)} custom-call(f32[1,128,128]{2,1,0:T(8,128)S(1)} %fusion.32), custom_call_target="Cholesky" | custom-call | tf_op jit(solution)/shard_map/while/body/eval_jaxpr/jit(cholesky)/cholesky | solution.py:35
  362.6 11.7 %custom-call.14 = f32[1,128,128]{2,1,0:T(8,128)S(1)} custom-call(f32[1,128,128]{2,1,0:T(8,128)S(1)} %fusion.32), custom_call_target="Cholesky" | custom-call | tf_op jit(solution)/shard_map/while/body/eval_jaxpr/jit(cholesky)/cholesky | solution.py:35
  377.3 11.7 %custom-call.14 = f32[1,128,128]{2,1,0:T(8,128)S(1)} custom-call(f32[1,128,128]{2,1,0:T(8,128)S(1)} %fusion.32), custom_call_target="Cholesky" | custom-call | tf_op jit(solution)/shard_map/while/body/eval_jaxpr/jit(cholesky)/cholesky | solution.py:35
  392.0 11.7 %custom-call.14 = f32[1,128,128]{2,1,0:T(8,128)S(1)} custom-call(f32[1,128,128]{2,1,0:T(8,128)S(1)} %fusion.32), custom_call_target="Cholesky" | custom-call | tf_op jit(solution)/shard_map/while/body/eval_jaxpr/jit(cholesky)/cholesky | solution.py:35
  406.7 11.7 %custom-call.14 = f32[1,128,128]{2,1,0:T(8,128)S(1)} custom-call(f32[1,128,128]{2,1,0:T(8,128)S(1)} %fusion.32), custom_call_target="Cholesky" | custom-call | tf_op jit(solution)/shard_map/while/body/eval_jaxpr/jit(cholesky)/cholesky | solution.py:35
  (293 shorter events, 274.3 us)
Async XLA Ops:
  7.2 118.2 %all-gather.3.cloned.1.call-start = ((), (), s32[]{:S(2)}) async-start(), calls=%async_computation.1 | async-start | bytes 2162688 | tf_op jit(solution)/shard_map/all_gather | solution.py:12
  7.9 18.4 %copy-start = (s32[16]{0:T(128)S(1)}, s32[16]{0:T(128)}, u32[]{:S(2)}) copy-start(s32[16]{0:T(128)} %param.10) | copy-start | bytes 196
Sparse Core Ops, SparseCore 0:
  69.9 55.3 all-gather.2
where the time goes:
time: 604 us; the launch traced here: 601 us
  other arithmetic  430 us (71%)
  waiting for transfers between devices  55.6 us (9%)
  matrix products  47.5 us (8%)
  blocking collectives  27.5 us (5%)
  local copies, waits for them, and re-layouts  24.5 us (4%)
  between operations  14.2 us (2%)
    another operation x96, other arithmetic, upper_of(): return jnp.swapaxes(jnp.linalg.cholesky(matrix), -1, -2)  396 us
    all_gather x1, waiting for transfers between devices, merged(): everything = lax.all_gather(value, axis)  55.5 us
    dot_general x31, matrix products, merge_pair(): jnp.einsum('fka,fkb->fab', second_r, second_r, precision=lax.Precision.HI...  37.4 us
    all_to_all x1, blocking collectives, local(): lax.all_to_all(spectra, 'blk', split_axis=0, concat_axis=2, tiled=True)  27.5 us
    transpose x32, other arithmetic, upper_of(): return jnp.swapaxes(jnp.linalg.cholesky(matrix), -1, -2)  21 us
    gather x24, local copies, waits for them, and re-layouts  18.3 us
  transfers between devices with their start and end apart: 1, of which 1 were waited for; matrix products, arithmetic and copies ran while one was open for 0% of the time, Pallas kernels for 0%

commit v1 on v0

v1 whole, which is shorter than its diff:
```python
import math

import jax
import jax.numpy as jnp
from jax import lax
from jax.sharding import PartitionSpec as P

NFFT = 512


def padded_coeffs(row_scales, block_offsets, freq_index):
    rows = row_scales.shape[0]
    times = jnp.arange(rows, dtype=jnp.int32)[None, :] - block_offsets[:, None]
    inside = (times >= 0) & (times < NFFT)
    hann = 0.5 - 0.5 * jnp.cos(2.0 * math.pi / NFFT * times.astype(jnp.float32))
    weight = jnp.where(inside, hann * row_scales[None, :], 0.0) / math.sqrt(NFFT)
    quarter = jnp.arange(2, dtype=jnp.int32) * (NFFT // 4)
    phase = freq_index[:, None, None, None] * times[None, :, None, :]
    phase = (phase + quarter[None, None, :, None]) & (NFFT - 1)
    table = jnp.cos(2.0 * math.pi / NFFT * phase.astype(jnp.float32))
    return (table * weight[None, :, None, :]).astype(jnp.bfloat16)


def local(snapshots, row_scales, block_offsets, freq_index):
    points_here = snapshots.shape[1]
    freq_count = freq_index.shape[0]
    blocks_here = block_offsets.shape[0]
    coeffs = padded_coeffs(row_scales, block_offsets, freq_index)
    coeffs = coeffs.reshape(freq_count * blocks_here * 2, -1)
    spectra = jnp.dot(coeffs, snapshots, preferred_element_type=jnp.float32)
    spectra = spectra.astype(jnp.bfloat16).reshape(freq_count, 2 * blocks_here, points_here)
    regrouped = lax.all_to_all(spectra, "blk", split_axis=0, concat_axis=1, tiled=True)
    rows = regrouped[0]
    total_points = points_here * lax.axis_size("space")
    product = jnp.dot(rows, rows.T, preferred_element_type=jnp.float32) / total_points
    product = lax.optimization_barrier(lax.psum(product, "space"))
    width = product.shape[0]
    quads = product.reshape(width // 2, 2, width // 2, 2)
    real = quads[:, 0, :, 0] + quads[:, 1, :, 1]
    imag = quads[:, 0, :, 1] - quads[:, 1, :, 0]
    gram = jnp.stack(
        [jnp.stack([real, imag], -1), jnp.stack([-imag, real], -1)], 1
    ).reshape(width, width)
    lower = jnp.linalg.cholesky(gram)
    identity = jnp.eye(width, dtype=jnp.float32)
    inverse_lower = jax.scipy.linalg.solve_triangular(lower, identity, lower=True)
    modes = lax.dot_general(
        rows.astype(jnp.float32),
        inverse_lower,
        (((0,), (1,)), ((), ())),
        precision=lax.Precision.HIGHEST,
    )
    upper = lower.T
    r_factor = jnp.stack([upper[0::2, 0::2], upper[0::2, 1::2]], 0)
    return (modes[None], r_factor[None])


def solution(mesh):
    return jax.shard_map(
        local,
        mesh=mesh,
        in_specs=(P("blk", "space"), P("blk"), P("blk"), P()),
        out_specs=(P("blk", "space", None), P("blk", None, None, None)),
        check_vma=False,
    )
```

time: 604 us -> 219 us (0.36)
  other arithmetic: 430 us -> 31.2 us
  waiting for transfers between devices: 55.6 us -> 125 us
  matrix products: 47.5 us -> 4.68 us
  local copies, waits for them, and re-layouts: 24.5 us -> 16.6 us
    another operation x100 -> x6, other arithmetic: 407 us -> 22.2 us  [the longest x3 12.4 us: local(): lower = jnp.linalg.cholesky(gram)]
    psum x0 -> x1, waiting for transfers between devices: none -> 124 us  [local(): product = lax.optimization_barrier(lax.psum(product, 'space'))]
    all_gather x1 -> x0, waiting for transfers between devices: 55.5 us -> none  [merged(): everything = lax.all_gather(value, axis)]
    dot_general x65 -> x3, matrix products: 47.2 us -> 4.43 us  [the longest x1 2.59 us: local(): spectra = jnp.dot(coeffs, snapshots, preferred_element_type=jnp.float32)]
    transpose x32 -> x1, other arithmetic: 21 us -> 0.66 us  [local(): upper = lower.T]
    gather x24 -> x0, local copies, waits for them, and re-layouts: 18.3 us -> none
    reshape x5 -> x3, local copies, waits for them, and re-layouts: 0.29 us -> 10.5 us  [the longest x1 6.24 us: local(): quads = product.reshape(width // 2, 2, width // 2, 2)]
    sub x1 -> x2, other arithmetic: 0.04 us -> 6.56 us  [the longest x1 5.74 us: local(): imag = quads[:, 0, :, 1] - quads[:, 1, :, 0]]
where the time goes in v1:
time: 219 us
  waiting for transfers between devices  125 us (57%)
  other arithmetic  31.2 us (14%)
  blocking collectives  27.5 us (13%)
  local copies, waits for them, and re-layouts  16.6 us (8%)
  between operations  14.2 us (6%)
  matrix products  4.68 us (2%)
    psum x1, waiting for transfers between devices, local(): product = lax.optimization_barrier(lax.psum(product, 'space'))  124 us
    all_to_all x1, blocking collectives, local(): lax.all_to_all(spectra, 'blk', split_axis=0, concat_axis=1, tiled=True)  27.5 us
    another operation x3, other arithmetic, local(): lower = jnp.linalg.cholesky(gram)  12.4 us
    another operation x1, other arithmetic, local(): jax.scipy.linalg.solve_triangular(lower, identity, lower=True)  9.81 us
    reshape x1, local copies, waits for them, and re-layouts, local(): quads = product.reshape(width // 2, 2, width // 2, 2)  6.24 us
    sub x1, other arithmetic, local(): imag = quads[:, 0, :, 1] - quads[:, 1, :, 0]  5.74 us
  transfers between devices with their start and end apart: 1, of which 1 were waited for; matrix products, arithmetic and copies ran while one was open for 0% of the time, Pallas kernels for 0%

profile of v1, /device:TPU:1, one launch (start us, length us, event | category | flops | bytes accessed | tf_op | source)
XLA Modules:
  0.0 218.7 jit_solution(5565477457189449705)
XLA Ops:
  7.2 0.8 iota_subtract_fusion
  8.1 0.9 select_multiply_fusion
  9.1 0.8 broadcast_multiply_fusion
  9.9 0.2 add.47
  10.2 0.5 add.48
  10.6 0.2 mul.83
  10.8 0.5 mul.84
  11.3 2.6 %fusion.2 = bf16[16,8,512]{2,1,0:T(8,128)(2,1)S(1)} fusion(bf16[1280,512]{1,0:T(8,128)(2,1)S(1)} %copy-done, f32[128,1280]{1,0:T(8,128)S(1)} %mul.84, s32[128,1280]{1,0:T(8,128)S(1)} %add.48, s32[128]{0:T(128)S(1)} %add.50), kind=kOutput, calls=%fused_computation.6 | convolution fusion | flops 168820736 | bytes 2753024 | tf_op jit(solution)/shard_map/dot_general | solution.py:30
  13.9 27.5 %all_to_all.4 = bf16[16,8,512]{2,1,0:T(8,128)(2,1)S(1)} all-to-all(bf16[16,8,512]{2,1,0:T(8,128)(2,1)S(1)} %fusion.2), channel_id=1, replica_groups=mesh['space'=32,'blk'=16] {'blk'}, dimensions={0} | all-to-all | bytes 262144 | tf_op jit(solution)/shard_map/all_to_all | solution.py:32
  41.4 0.8 convolution_multiply_fusion
  42.2 124.5 %all-reduce.2.cloned.1.call-done = f32[128,128]{1,0:T(8,128)} async-done(((f32[128,128]{1,0:T(8,128)}), f32[128,128]{1,0:T(8,128)}) %all-reduce.2.cloned.1.call-update) | async-done | bytes 65552 | tf_op jit(solution)/shard_map/psum | solution.py:36
  166.7 6.2 %reshape.147 = f32[64,2,64,2]{3,2,1,0:T(8,128)} reshape(f32[128,128]{1,0:T(8,128)} %all-reduce.2.cloned.1.call-done) | data formatting | bytes 131072 | tf_op jit(solution)/shard_map/reshape | solution.py:38
  173.0 5.7 %fusion = (f32[64,64]{1,0:T(8,128)S(1)}, f32[64,64]{1,0:T(8,128)S(1)}) fusion(f32[64,2,64,2]{3,2,1,0:T(8,128)} %reshape.147), kind=kLoop, calls=%fused_computation.1 | loop fusion | flops 8192 | bytes 98304 | tf_op jit(solution)/shard_map/sub | solution.py:40
  178.8 2.7 %copy.21 = f32[64,2,64,2]{3,2,1,0:T(8,128)} copy(f32[64,2,64,2]{2,0,3,1:T(8,128)S(1)} %pad_maximum_fusion) | data formatting | bytes 131072 | tf_op jit(solution)/shard_map/stack | solution.py:41
  181.5 4.2 %reshape.148 = f32[128,128]{1,0:T(8,128)S(1)} reshape(f32[64,2,64,2]{3,2,1,0:T(8,128)} %copy.21) | data formatting | bytes 131072 | tf_op jit(solution)/shard_map/reshape | solution.py:43
  185.8 11.7 %cholesky.17 = f32[128,128]{1,0:T(8,128)S(1)} custom-call(f32[128,128]{1,0:T(8,128)S(1)} %fusion.10), custom_call_target="Cholesky" | custom-call | tf_op jit(solution)/shard_map/jit(cholesky)/cholesky | solution.py:44
  197.5 0.6 compare_reduce_fusion
  198.2 0.7 fusion.11
  198.8 0.6 slice.35
  199.4 0.6 slice.34
  200.0 9.8 %custom-call.7 = f32[1,128,128]{1,2,0:T(8,128)S(1)} custom-call(f32[1,128,128]{2,1,0:T(8,128)S(1)} %get-tuple-element.13), custom_call_target="InvertDiagBlocksLowerTriangular" | custom-call | tf_op jit(solution)/shard_map/jit(_solve_triangular)/triangular_solve | solution.py:46
  209.9 0.2 fusion.8
  210.1 0.7 copy.23
  210.8 1.0 convolution_bitcast_fusion
  (14 shorter events, 0.4 us)
Async XLA Ops:
  7.2 4.1 %copy-start = (bf16[1280,512]{1,0:T(8,128)(2,1)S(1)}, bf16[1280,512]{1,0:T(8,128)(2,1)}, u32[]{:S(2)}) copy-start(bf16[1280,512]{1,0:T(8,128)(2,1)} %param.4) | copy-start | bytes 3932164
  7.2 159.5 %all-reduce.2.cloned.1.call-start = ((), (), s32[]{:S(2)}) async-start(), calls=%async_computation.1 | async-start | bytes 131072 | tf_op jit(solution)/shard_map/psum | solution.py:36
Sparse Core Ops, SparseCore 0:
  42.3 124.3 all-reduce.1

commit v2 on v1

v2 whole, which is shorter than its diff:
```python
import functools
import math

import jax
import jax.numpy as jnp
from jax import lax
from jax.experimental import pallas as pl
from jax.experimental.pallas import tpu as pltpu
from jax.sharding import PartitionSpec as P

NFFT = 512
TILE = 8
LANES = 128
MESH = pl.DeviceIdType.MESH


def cos_turns(turns):
    frac = turns - jnp.floor(turns + 0.5)
    half = frac * math.pi
    sq = half * half
    poly = 1.0 + sq * (
        -1.0 / 6
        + sq
        * (
            1.0 / 120
            + sq * (-1.0 / 5040 + sq * (1.0 / 362880 + sq * (-1.0 / 39916800 + sq * (1.0 / 6227020800))))
        )
    )
    sine = half * poly
    return 1.0 - 2.0 * (sine * sine)


def grid_of(space):
    side = {32: 4, 8: 2}[space]
    return side, side


def gather_kernel(
    sides, zs, total_points,
    snaps_hbm, scales_ref, offs_ref, freq_ref,
    xy_ref, gram_ref,
    snaps, coef, send, recv, rows32, pair_buf, x_buf, y_buf,
    load_sem, send_sems, recv_sems, gsend_sems, grecv_sems,
):
    ys, xs = sides
    z = lax.axis_index("blk")
    s = lax.axis_index("space")
    core = lax.rem(s, 2)
    x = lax.rem(s // 2, xs)
    y = s // (2 * xs)

    load = pltpu.make_async_copy(snaps_hbm, snaps, load_sem)
    load.start()

    def space_of(yy, xx, cc):
        return (yy * xs + xx) * 2 + cc

    z_peers = [lax.rem(z + d, zs) for d in range(1, zs)]
    x_peers = [space_of(y, lax.rem(x + d, xs), core) for d in range(1, xs)]
    y_peers = [space_of(lax.rem(y + d, ys), x, core) for d in range(1, ys)]
    pair = space_of(y, x, 1 - core)

    barrier = pltpu.get_barrier_semaphore()
    for peer in z_peers:
        pl.semaphore_signal(barrier, inc=1, device_id={"blk": peer}, device_id_type=MESH)
    for peer in [pair] + x_peers + y_peers:
        pl.semaphore_signal(barrier, inc=1, device_id={"space": peer}, device_id_type=MESH)

    rows = snaps.shape[0]
    freqs = freq_ref.shape[0]
    sub = lax.broadcasted_iota(jnp.int32, (TILE, rows), 0)
    times = lax.broadcasted_iota(jnp.int32, (TILE, rows), 1)
    start = jnp.full((TILE, rows), offs_ref[0], jnp.int32)
    for b in range(1, TILE // 2):
        start = jnp.where(sub >= 2 * b, offs_ref[b], start)
    times = times - start
    ftimes = times.astype(jnp.float32)
    hann = 0.5 - 0.5 * cos_turns(ftimes * (1.0 / NFFT))
    inside = (times >= 0) & (times < NFFT)
    weight = jnp.where(inside, hann * scales_ref[...], 0.0) * (1.0 / math.sqrt(NFFT))
    quarter = (sub & 1).astype(jnp.float32) * 0.25

    def rows_of(j):
        turns = ftimes * (freq_ref[j].astype(jnp.float32) * (1.0 / NFFT)) + quarter
        return cos_turns(turns) * weight

    @pl.loop(0, freqs // 2)
    def _(jj):
        both = jnp.concatenate([rows_of(2 * jj), rows_of(2 * jj + 1)], 0)
        coef[pl.ds(pl.multiple_of(jj * 16, 16), 16), :] = both.astype(jnp.bfloat16)

    load.wait()
    spectra = jnp.dot(coef[...], snaps[...], preferred_element_type=jnp.float32)
    send[...] = spectra.reshape(send.shape).astype(jnp.bfloat16)
    recv[z] = send[z]

    pl.semaphore_wait(barrier, len(z_peers) + 1 + len(x_peers) + len(y_peers))
    order = sorted(range(1, zs), key=lambda d: -min(d, zs - d))
    copies = []
    for d in order:
        peer = z_peers[d - 1]
        copy = pltpu.make_async_remote_copy(
            src_ref=send.at[peer],
            dst_ref=recv.at[z],
            send_sem=send_sems.at[d],
            recv_sem=recv_sems.at[d],
            device_id={"blk": peer},
            device_id_type=MESH,
        )
        copy.start()
        copies.append(copy)
    for copy in copies:
        copy.wait_recv()
    points = recv.shape[2]
    half = zs * TILE // 2
    chunks = range(points // LANES)
    for q in chunks:
        part = recv[:, :, LANES * q : LANES * (q + 1)].astype(jnp.float32)
        rows32[q] = part.reshape(2 * half, LANES)

    def every_other(first):
        parts = [rows32[q, pl.ds(first, half, stride=2), :] for q in chunks]
        return jnp.concatenate(parts, 1).astype(jnp.bfloat16)

    re, im = every_other(0), every_other(1)
    xy_ref[pl.ds(0, half), :] = re
    xy_ref[pl.ds(half, half), :] = im
    left = jnp.concatenate([re, im], 1)
    right = jnp.concatenate([left, jnp.concatenate([im, -re], 1)], 0)
    gram = lax.dot_general(
        left, right, (((1,), (1,)), ((), ())), preferred_element_type=jnp.float32
    )
    pair_buf[core] = gram
    for copy in copies:
        copy.wait_send()

    def exchange(buf, here, peers, base):
        moves = []
        for i, peer in enumerate(peers):
            move = pltpu.make_async_remote_copy(
                src_ref=buf.at[here],
                dst_ref=buf.at[here],
                send_sem=gsend_sems.at[base + i],
                recv_sem=grecv_sems.at[base + i],
                device_id={"space": peer},
                device_id_type=MESH,
            )
            move.start()
            moves.append(move)
        for move in moves:
            move.wait()
        total = buf[0]
        for i in range(1, buf.shape[0]):
            total = total + buf[i]
        return total

    x_buf[x] = exchange(pair_buf, core, [pair], 0)
    y_buf[y] = exchange(x_buf, x, x_peers, 1)
    gram_ref[...] = exchange(y_buf, y, y_peers, xs) * (1.0 / total_points)


def gather_call(snapshots, scales, offsets, freqs, *, space, zs):
    sides = grid_of(space)
    points = snapshots.shape[1]
    cols = zs * TILE
    kernel = functools.partial(gather_kernel, sides, zs, points * space)
    gram_shape = (cols // 2, cols)
    vmem = pl.BlockSpec(memory_space=pltpu.VMEM)
    smem = pl.BlockSpec(memory_space=pltpu.SMEM)
    return pl.pallas_call(
        kernel,
        out_shape=(
            jax.ShapeDtypeStruct((cols, points), jnp.bfloat16),
            jax.ShapeDtypeStruct(gram_shape, jnp.float32),
        ),
        in_specs=[pl.BlockSpec(memory_space=pl.ANY), vmem, smem, smem],
        out_specs=(vmem, vmem),
        scratch_shapes=[
            pltpu.VMEM(snapshots.shape, jnp.bfloat16),
            pltpu.VMEM((zs * TILE, snapshots.shape[0]), jnp.bfloat16),
            pltpu.VMEM((zs, TILE, points), jnp.bfloat16),
            pltpu.VMEM((zs, TILE, points), jnp.bfloat16),
            pltpu.VMEM((points // LANES, cols, LANES), jnp.float32),
            pltpu.VMEM((2,) + gram_shape, jnp.float32),
            pltpu.VMEM((sides[1],) + gram_shape, jnp.float32),
            pltpu.VMEM((sides[0],) + gram_shape, jnp.float32),
            pltpu.SemaphoreType.DMA(()),
            pltpu.SemaphoreType.DMA((zs,)),
            pltpu.SemaphoreType.DMA((zs,)),
            pltpu.SemaphoreType.DMA((sum(sides),)),
            pltpu.SemaphoreType.DMA((sum(sides),)),
        ],
        compiler_params=pltpu.CompilerParams(collective_id=0, has_side_effects=True),
        name="spectra_and_gram",
    )(snapshots, scales, offsets, freqs)


def factor_kernel(xy_ref, gram_ref, modes_ref, r_ref, w_ref):
    n = gram_ref.shape[0]
    width = 2 * n
    tiles = n // TILE
    lane = lax.broadcasted_iota(jnp.int32, (TILE, width), 1)
    sub = lax.broadcasted_iota(jnp.int32, (TILE, width), 0)
    sign = jnp.where(lane < n, -1.0, 1.0)

    def turn(value):
        return pltpu.roll(value, n, 1) * sign

    def spread(value, row):
        return jnp.broadcast_to(value[row : row + 1, :], (TILE, width))

    def across(value, column):
        return jnp.broadcast_to(value[:, column : column + 1], (TILE, width))

    cs = [gram_ref[pl.ds(TILE * i, TILE), :] for i in range(tiles)]
    ls = [jnp.where(lane == sub + TILE * i, 1.0, 0.0) for i in range(tiles)]

    for panel in range(tiles):
        group = [panel] + ([panel + 1] if panel + 1 < tiles else [])
        res = {i: [across(cs[i], TILE * panel + j) for j in range(TILE)] for i in group}
        ims = {i: [across(cs[i], n + TILE * panel + j) for j in range(TILE)] for i in group}
        scale = jnp.zeros((TILE, width), jnp.float32)
        for k in range(TILE):
            pivot = spread(res[panel][k], k)
            inverse = 1.0 / pivot
            scale = jnp.where(sub == k, lax.rsqrt(pivot), scale)
            mults = {}
            for i in group:
                mr, mi = res[i][k] * inverse, ims[i][k] * inverse
                if i == panel:
                    mr = jnp.where(sub > k, mr, 0.0)
                    mi = jnp.where(sub > k, mi, 0.0)
                mults[i] = (mr, mi)
            for j in range(k + 1, TILE):
                pr, pi = spread(res[panel][j], k), spread(ims[panel][j], k)
                for i in group:
                    mr, mi = mults[i]
                    res[i][j] = res[i][j] - (mr * pr - mi * pi)
                    ims[i][j] = ims[i][j] - (mr * pi + mi * pr)
            c_row, l_row = spread(cs[panel], k), spread(ls[panel], k)
            c_turn, l_turn = turn(c_row), turn(l_row)
            for i in group:
                mr, mi = mults[i]
                cs[i] = cs[i] - (mr * c_row + mi * c_turn)
                ls[i] = ls[i] - (mr * l_row + mi * l_turn)
        r_rows = cs[panel] * scale
        l_rows = ls[panel] * scale
        if panel + 2 < tiles:
            first = TILE * (panel + 2)
            lhs = jnp.concatenate([r_rows, pltpu.roll(r_rows, n, 1)], 0)
            rhs = jnp.concatenate(
                [
                    jnp.concatenate([r_rows, l_rows], 1),
                    jnp.concatenate([-turn(r_rows), -turn(l_rows)], 1),
                ],
                0,
            )
            update = lax.dot_general(
                lhs[:, :n],
                rhs,
                (((0,), (0,)), ((), ())),
                precision=lax.Precision.HIGHEST,
                preferred_element_type=jnp.float32,
            )
            for i in range(panel + 2, tiles):
                part = update[TILE * i : TILE * (i + 1), :]
                cs[i] = cs[i] - part[:, :width]
                ls[i] = ls[i] - part[:, width:]
        row = sub + TILE * panel
        keep = (lane >= row) & ((lane < n) | (lane - n > row))
        r_rows = jnp.where(keep, r_rows, 0.0)
        r_ref[0, pl.ds(TILE * panel, TILE), :] = r_rows[:, :n]
        r_ref[1, pl.ds(TILE * panel, TILE), :] = pltpu.roll(r_rows, n, 1)[:, :n]
        w_ref[pl.ds(2 * TILE * panel, TILE, stride=2), :] = l_rows
        w_ref[pl.ds(2 * TILE * panel + 1, TILE, stride=2), :] = turn(l_rows)

    w = w_ref[...]
    high = w.astype(jnp.bfloat16)
    low = (w - high.astype(jnp.float32)).astype(jnp.bfloat16)
    xy = xy_ref[...]
    dims = (((0,), (1,)), ((), ()))
    modes = lax.dot_general(xy, high, dims, preferred_element_type=jnp.float32)
    modes += lax.dot_general(xy, low, dims, preferred_element_type=jnp.float32)
    modes_ref[...] = modes


def factor_call(xy, gram):
    n = gram.shape[0]
    return pl.pallas_call(
        factor_kernel,
        out_shape=(
            jax.ShapeDtypeStruct((xy.shape[1], 2 * n), jnp.float32),
            jax.ShapeDtypeStruct((2, n, n), jnp.float32),
        ),
        scratch_shapes=[pltpu.VMEM((2 * n, 2 * n), jnp.float32)],
        name="factor_and_modes",
    )(xy, gram)


def local(space, zs, snapshots, row_scales, block_offsets, freq_index):
    xy, gram = gather_call(
        snapshots, row_scales[None, :], block_offsets, freq_index, space=space, zs=zs
    )
    modes, r_factor = factor_call(xy, gram)
    return (modes[None], r_factor[None])


def solution(mesh):
    return jax.shard_map(
        functools.partial(local, mesh.shape["space"], mesh.shape["blk"]),
        mesh=mesh,
        in_specs=(P("blk", "space"), P("blk"), P("blk"), P()),
        out_specs=(P("blk", "space", None), P("blk", None, None, None)),
        check_vma=False,
    )
```

time: 219 us -> 45.3 us (0.21)
  waiting for transfers between devices: 125 us -> 0 us
  Pallas kernels: 0 us -> 43.1 us
  other arithmetic: 31.2 us -> 0 us
  blocking collectives: 27.5 us -> 0 us
  local copies, waits for them, and re-layouts: 16.6 us -> 1.29 us
  between operations: 14.2 us -> 0.64 us
  matrix products: 4.68 us -> 0 us
    psum x1 -> x0, waiting for transfers between devices: 124 us -> none  [local(): product = lax.optimization_barrier(lax.psum(product, 'space'))]
    pallas_call x0 -> x2, Pallas kernels: none -> 43.1 us  [the longest x1 36.2 us: gather_call(): pl.pallas_call(kernel, out_shape=(jax.ShapeDtypeStruct((cols, points), jn...]
    all_to_all x1 -> x0, blocking collectives: 27.5 us -> none  [local(): lax.all_to_all(spectra, 'blk', split_axis=0, concat_axis=1, tiled=True)]
    another operation x6 -> x0, other arithmetic: 22.2 us -> none  [the longest x3 12.4 us: local(): lower = jnp.linalg.cholesky(gram)]
    reshape x3 -> x0, local copies, waits for them, and re-layouts: 10.5 us -> none  [the longest x1 6.24 us: local(): quads = product.reshape(width // 2, 2, width // 2, 2)]
    sub x2 -> x0, other arithmetic: 6.56 us -> none  [the longest x1 5.74 us: local(): imag = quads[:, 0, :, 1] - quads[:, 1, :, 0]]
    dot_general x3 -> x0, matrix products: 4.43 us -> none  [the longest x1 2.59 us: local(): spectra = jnp.dot(coeffs, snapshots, preferred_element_type=jnp.float32)]
    another operation x1 -> x0, local copies, waits for them, and re-layouts: 2.71 us -> none  [local(): jnp.stack([jnp.stack([real, imag], -1), jnp.stack([-imag, real], -1)], 1)]
  transfers between devices with their start and end apart: 1 -> 0, of which waited for: 1 -> 0; matrix products, arithmetic and copies ran while one was open for 0% -> 0% of each run, Pallas kernels for 0% -> 0%
where the time goes in v2:
time: 45.3 us; the launch traced here: 45 us
  Pallas kernels  43.1 us (95%)
  local copies, waits for them, and re-layouts  1.29 us (3%)
  between operations  0.64 us (1%)
    pallas_call x1, Pallas kernels, gather_call(): pl.pallas_call(kernel, out_shape=(jax.ShapeDtypeStruct((cols, points), jn...  36.2 us
    pallas_call x1, Pallas kernels, factor_call(): pl.pallas_call(factor_kernel, out_shape=(jax.ShapeDtypeStruct((xy.shape[1...  6.94 us
    broadcast_in_dim x1, local copies, waits for them, and re-layouts, local(): row_scales[None, :]  1.29 us

profile of v2, /device:TPU:1, one launch (start us, length us, event | category | flops | bytes accessed | tf_op | source)
XLA Modules:
  0.0 45.0 jit_solution(15773448737632493756)
XLA Ops:
  0.6 1.3 %broadcast_in_dim.9.scales_ref = f32[1,1280]{1,0:T(1,128)} reshape(f32[1280]{0:T(1024)} %param.5) | data formatting | bytes 10240 | tf_op jit(solution)/shard_map/broadcast_in_dim | solution.py:302
  1.9 36.2 %spectra_and_gram.1 = (bf16[128,512]{1,0:T(8,128)(2,1)}, f32[64,128]{1,0:T(8,128)}) custom-call(bf16[1280,512]{1,0:T(8,128)(2,1)} %snaps_hbm.1, f32[1,1280]{1,0:T(1,128)} %broadcast_in_dim.9.scales_ref, s32[4]{0:T(128)} %offs_ref.1, s32[16]{0:T(128)} %freq_ref.1), custom_call_target="tpu_custom_call" | custom-call | tf_op jit(solution)/shard_map/spectra_and_gram/pallas_call | solution.py:170
  38.1 6.9 %factor_and_modes.1 = (f32[512,128]{1,0:T(8,128)}, f32[2,64,64]{2,1,0:T(8,128)}) custom-call(bf16[128,512]{1,0:T(8,128)(2,1)} %get-tuple-element.6.xy_ref, f32[64,128]{1,0:T(8,128)} %get-tuple-element.7.gram_ref), custom_call_target="tpu_custom_call" | custom-call | tf_op jit(solution)/shard_map/factor_and_modes/pallas_call | solution.py:289

commit v3 on v2

v3 whole, which is shorter than its diff:
```python
import functools
import math

import jax
import jax.numpy as jnp
from jax import lax
from jax.experimental import pallas as pl
from jax.experimental.pallas import tpu as pltpu
from jax.sharding import PartitionSpec as P

NFFT = 512
TILE = 8
LANES = 128
PARTS = 1
MESH = pl.DeviceIdType.MESH


def cos_turns(turns):
    frac = turns - jnp.floor(turns + 0.5)
    half = frac * math.pi
    sq = half * half
    poly = 1.0 + sq * (
        -1.0 / 6
        + sq
        * (
            1.0 / 120
            + sq * (-1.0 / 5040 + sq * (1.0 / 362880 + sq * (-1.0 / 39916800 + sq * (1.0 / 6227020800))))
        )
    )
    sine = half * poly
    return 1.0 - 2.0 * (sine * sine)


def sides_of(space):
    side = {32: 4, 8: 2}[space]
    return side, side


def iota(shape, axis):
    return lax.broadcasted_iota(jnp.int32, shape, axis)


def write_coeffs(scales_ref, offs_ref, freq_ref, coef, table, phase):
    rows = scales_ref.shape[0]
    freqs = freq_ref.shape[0]
    tile = (TILE, LANES)
    sub, lane = iota(tile, 0), iota(tile, 1)
    start = jnp.full(tile, offs_ref[0], jnp.int32)
    for b in range(1, TILE // 2):
        start = jnp.where(sub >= 2 * b, offs_ref[b], start)

    high = (freqs + TILE - 1) // TILE * TILE
    down = jnp.zeros((high, LANES), jnp.float32)
    along = jnp.zeros(tile, jnp.float32)
    for j in range(freqs):
        freq = freq_ref[j].astype(jnp.float32) * (1.0 / NFFT)
        down = jnp.where(iota((high, LANES), 0) == j, freq, down)
        along = jnp.where(lane == j, freq, along)
    for q in range(NFFT // LANES):
        turns = down * (iota((high, LANES), 1) + LANES * q).astype(jnp.float32)
        table[0, q] = cos_turns(turns)
        table[1, q] = cos_turns(turns + 0.25)
    turns = (sub & 1).astype(jnp.float32) * 0.25 - along * start.astype(jnp.float32)
    cos_part, sin_part = cos_turns(turns), cos_turns(turns + 0.25)
    for j in range(freqs):
        phase[0, j] = jnp.broadcast_to(cos_part[:, j : j + 1], tile)
        phase[1, j] = jnp.broadcast_to(sin_part[:, j : j + 1], tile)

    weights = []
    for q in range(rows // LANES):
        times = lane + LANES * q - start
        hann = 0.5 - 0.5 * cos_turns(times.astype(jnp.float32) * (1.0 / NFFT))
        scale = scales_ref[pl.ds(LANES * q, LANES)]
        inside = (times >= 0) & (times < NFFT)
        weight = jnp.where(inside, hann * scale[None, :], 0.0)
        weights.append(weight * (1.0 / math.sqrt(NFFT)))

    @pl.loop(0, freqs // 2)
    def _(pair):
        for q in range(rows // LANES):
            turn = q % (NFFT // LANES)
            parts = []
            for j in (2 * pair, 2 * pair + 1):
                cosine = table[0, turn, pl.ds(j, 1), :]
                sine = table[1, turn, pl.ds(j, 1), :]
                value = cosine * phase[0, j] - sine * phase[1, j]
                parts.append(value * weights[q])
            both = jnp.concatenate(parts, 0).astype(jnp.bfloat16)
            coef[pl.ds(pl.multiple_of(pair * 16, 16), 16), pl.ds(LANES * q, LANES)] = both


def gather_kernel(
    sides, zs, total_points,
    snaps_hbm, scales_hbm, offs_hbm, freq_hbm,
    xy, gram_ref,
    snaps, scales_ref, offs_ref, freq_ref, coef, table, phase, send, recv, rows32,
    pair_buf, x_buf, y_buf,
    load_sems, send_sems, recv_sems, gsend_sems, grecv_sems,
):
    ys, xs = sides
    z = lax.axis_index("blk")
    s = lax.axis_index("space")
    core = lax.rem(s, 2)
    x = lax.rem(s // 2, xs)
    y = s // (2 * xs)

    loads = [
        pltpu.make_async_copy(source, target, load_sems.at[i])
        for i, (source, target) in enumerate(
            [
                (scales_hbm, scales_ref),
                (offs_hbm, offs_ref),
                (freq_hbm, freq_ref),
                (snaps_hbm, snaps),
            ]
        )
    ]
    for load in loads:
        load.start()

    def space_of(yy, xx, cc):
        return (yy * xs + xx) * 2 + cc

    z_peers = [lax.rem(z + d, zs) for d in range(1, zs)]
    x_peers = [space_of(y, lax.rem(x + d, xs), core) for d in range(1, xs)]
    y_peers = [space_of(lax.rem(y + d, ys), x, core) for d in range(1, ys)]
    pair = space_of(y, x, 1 - core)

    barrier = pltpu.get_barrier_semaphore()
    order = sorted(range(1, zs), key=lambda d: -min(d, zs - d))
    for d in order:
        peer = z_peers[d - 1]
        pl.semaphore_signal(barrier, inc=1, device_id={"blk": peer}, device_id_type=MESH)
    for peer in [pair] + x_peers + y_peers:
        pl.semaphore_signal(barrier, inc=1, device_id={"space": peer}, device_id_type=MESH)

    for load in loads[:3]:
        load.wait()
    write_coeffs(scales_ref, offs_ref, freq_ref, coef, table, phase)
    loads[3].wait()
    width = recv.shape[3]
    copies = []
    for h in range(PARTS):
        spectra = jnp.dot(
            coef[...], snaps[:, width * h : width * (h + 1)], preferred_element_type=jnp.float32
        )
        send[h] = spectra.reshape(send.shape[1:]).astype(jnp.bfloat16)
        recv[h, z] = send[h, z]
        if h == 0:
            pl.semaphore_wait(barrier, len(z_peers) + 1 + len(x_peers) + len(y_peers))
        for d in order:
            peer = z_peers[d - 1]
            copy = pltpu.make_async_remote_copy(
                src_ref=send.at[h, peer],
                dst_ref=recv.at[h, z],
                send_sem=send_sems.at[h, d],
                recv_sem=recv_sems.at[h, d],
                device_id={"blk": peer},
                device_id_type=MESH,
            )
            copy.start()
            copies.append(copy)

    half = zs * TILE // 2
    gram = jnp.zeros((half, 2 * half), jnp.float32)
    for h in range(PARTS):
        for copy in copies[(zs - 1) * h : (zs - 1) * (h + 1)]:
            copy.wait_recv()
        chunks = range(width // LANES)
        for q in chunks:
            part = recv[h, :, :, LANES * q : LANES * (q + 1)].astype(jnp.float32)
            rows32[h, q] = part.reshape(2 * half, LANES)

        def every_other(first):
            parts = [rows32[h, q, pl.ds(first, half, stride=2), :] for q in chunks]
            return jnp.concatenate(parts, 1).astype(jnp.bfloat16)

        re, im = every_other(0), every_other(1)
        left = jnp.concatenate([re, im], 1)
        right = jnp.concatenate([left, jnp.concatenate([im, -re], 1)], 0)
        gram += lax.dot_general(
            left, right, (((1,), (1,)), ((), ())), preferred_element_type=jnp.float32
        )
        xy[pl.ds(0, half), pl.ds(width * h, width)] = re
        xy[pl.ds(half, half), pl.ds(width * h, width)] = im

    row, lane = iota(gram.shape, 0), iota(gram.shape, 1)
    packed = jnp.where(lane >= row, gram, pltpu.roll(gram, half, 1))
    upper, lower = packed[: half // 2], pltpu.roll(packed[half // 2 :], half, 1)
    pair_buf[core] = jnp.where(iota(upper.shape, 1) < half, upper, lower)

    def exchange(buf, here, peers, base):
        moves = []
        for i, peer in enumerate(peers):
            move = pltpu.make_async_remote_copy(
                src_ref=buf.at[here],
                dst_ref=buf.at[here],
                send_sem=gsend_sems.at[base + i],
                recv_sem=grecv_sems.at[base + i],
                device_id={"space": peer},
                device_id_type=MESH,
            )
            move.start()
            moves.append(move)
        return moves

    def summed(buf, moves):
        for move in moves:
            move.wait_recv()
        total = buf[0]
        for i in range(1, buf.shape[0]):
            total = total + buf[i]
        return total

    moves_p = exchange(pair_buf, core, [pair], 0)
    x_buf[x] = summed(pair_buf, moves_p)
    moves_x = exchange(x_buf, x, x_peers, 1)
    y_buf[y] = summed(x_buf, moves_x)
    moves_y = exchange(y_buf, y, y_peers, xs)
    for copy in copies + moves_p + moves_x:
        copy.wait_send()
    gram_ref[...] = summed(y_buf, moves_y) * (1.0 / total_points)
    for move in moves_y:
        move.wait_send()


def gather_call(snapshots, scales, offsets, freqs, *, space, zs):
    sides = sides_of(space)
    rows, points = snapshots.shape
    cols = zs * TILE
    width = points // PARTS
    kernel = functools.partial(gather_kernel, sides, zs, points * space)
    gram_shape = (cols // 4, cols)
    vmem = pl.BlockSpec(memory_space=pltpu.VMEM)
    anywhere = pl.BlockSpec(memory_space=pl.ANY)
    high = (zs + TILE - 1) // TILE * TILE
    return pl.pallas_call(
        kernel,
        out_shape=(
            pltpu.VMEM((cols, points), jnp.bfloat16),
            pltpu.VMEM(gram_shape, jnp.float32),
        ),
        in_specs=[anywhere] * 4,
        out_specs=(vmem, vmem),
        scratch_shapes=[
            pltpu.VMEM(snapshots.shape, jnp.bfloat16),
            pltpu.VMEM(scales.shape, jnp.float32),
            pltpu.SMEM(offsets.shape, jnp.int32),
            pltpu.SMEM(freqs.shape, jnp.int32),
            pltpu.VMEM((zs * TILE, rows), jnp.bfloat16),
            pltpu.VMEM((2, NFFT // LANES, high, LANES), jnp.float32),
            pltpu.VMEM((2, zs, TILE, LANES), jnp.float32),
            pltpu.VMEM((PARTS, zs, TILE, width), jnp.bfloat16),
            pltpu.VMEM((PARTS, zs, TILE, width), jnp.bfloat16),
            pltpu.VMEM((PARTS, width // LANES, cols, LANES), jnp.float32),
            pltpu.VMEM((2,) + gram_shape, jnp.float32),
            pltpu.VMEM((sides[1],) + gram_shape, jnp.float32),
            pltpu.VMEM((sides[0],) + gram_shape, jnp.float32),
            pltpu.SemaphoreType.DMA((4,)),
            pltpu.SemaphoreType.DMA((PARTS, zs)),
            pltpu.SemaphoreType.DMA((PARTS, zs)),
            pltpu.SemaphoreType.DMA((sum(sides),)),
            pltpu.SemaphoreType.DMA((sum(sides),)),
        ],
        compiler_params=pltpu.CompilerParams(collective_id=0, has_side_effects=True),
        name="spectra_and_gram",
    )(snapshots, scales, offsets, freqs)


def unpacked(packed, n):
    both = jnp.concatenate([packed, pltpu.roll(packed, n, 1)], 0)
    flipped = both.T
    flipped = flipped[:n, :]
    row, lane = iota((n, n), 0), iota((n, n), 1)
    both = both[:, :n]
    real = jnp.where(lane >= row, both, flipped)
    imag = jnp.where(lane < row, both, jnp.where(lane > row, -flipped, 0.0))
    return jnp.concatenate([real, imag], 1)


def factor_kernel(xy, packed_ref, modes_ref, r_ref, w_ref):
    width = packed_ref.shape[1]
    n = width // 2
    tiles = n // TILE
    gram = unpacked(packed_ref[...], n)
    lane, sub = iota((TILE, width), 1), iota((TILE, width), 0)
    sign = jnp.where(lane < n, -1.0, 1.0)

    def turn(value):
        return pltpu.roll(value, n, 1) * sign

    def spread(value, row):
        return jnp.broadcast_to(value[row : row + 1, :], (TILE, width))

    def across(value, column):
        return jnp.broadcast_to(value[:, column : column + 1], (TILE, width))

    cs = [gram[TILE * i : TILE * (i + 1), :] for i in range(tiles)]
    ls = [jnp.where(lane == sub + TILE * i, 1.0, 0.0) for i in range(tiles)]

    for panel in range(tiles):
        group = [panel] + ([panel + 1] if panel + 1 < tiles else [])
        res = {i: [across(cs[i], TILE * panel + j) for j in range(TILE)] for i in group}
        ims = {i: [across(cs[i], n + TILE * panel + j) for j in range(TILE)] for i in group}
        scale = jnp.zeros((TILE, width), jnp.float32)
        for k in range(TILE):
            pivot = spread(res[panel][k], k)
            inverse = 1.0 / pivot
            scale = jnp.where(sub == k, lax.rsqrt(pivot), scale)
            mults = {i: (res[i][k] * inverse, ims[i][k] * inverse) for i in group}
            for j in range(k + 1, TILE):
                pr, pi = spread(res[panel][j], k), spread(ims[panel][j], k)
                for i in group:
                    mr, mi = mults[i]
                    res[i][j] = res[i][j] - (mr * pr - mi * pi)
                    ims[i][j] = ims[i][j] - (mr * pi + mi * pr)
            c_row, l_row = spread(cs[panel], k), spread(ls[panel], k)
            c_turn, l_turn = turn(c_row), turn(l_row)
            for i in group:
                mr, mi = mults[i]
                if i == panel:
                    mr, mi = jnp.where(sub > k, mr, 0.0), jnp.where(sub > k, mi, 0.0)
                cs[i] = cs[i] - (mr * c_row + mi * c_turn)
                ls[i] = ls[i] - (mr * l_row + mi * l_turn)
        r_rows = cs[panel] * scale
        l_rows = ls[panel] * scale
        if panel + 2 < tiles:
            first = TILE * (panel + 2)
            lhs = jnp.concatenate([r_rows, pltpu.roll(r_rows, n, 1)], 0)
            rhs = jnp.concatenate(
                [
                    jnp.concatenate([r_rows, l_rows], 1),
                    jnp.concatenate([-turn(r_rows), -turn(l_rows)], 1),
                ],
                0,
            )
            update = lax.dot_general(
                lhs[:, :n],
                rhs,
                (((0,), (0,)), ((), ())),
                precision=lax.Precision.HIGHEST,
                preferred_element_type=jnp.float32,
            )
            for i in range(panel + 2, tiles):
                part = update[TILE * i : TILE * (i + 1), :]
                cs[i] = cs[i] - part[:, :width]
                ls[i] = ls[i] - part[:, width:]
        row = sub + TILE * panel
        keep = (lane >= row) & ((lane < n) | (lane - n > row))
        r_rows = jnp.where(keep, r_rows, 0.0)
        r_ref[0, pl.ds(TILE * panel, TILE), :] = r_rows[:, :n]
        r_ref[1, pl.ds(TILE * panel, TILE), :] = pltpu.roll(r_rows, n, 1)[:, :n]
        w_ref[pl.ds(2 * TILE * panel, TILE, stride=2), :] = l_rows
        w_ref[pl.ds(2 * TILE * panel + 1, TILE, stride=2), :] = turn(l_rows)

    w = w_ref[...]
    high = w.astype(jnp.bfloat16)
    low = (w - high.astype(jnp.float32)).astype(jnp.bfloat16)
    points = xy[...]
    dims = (((0,), (1,)), ((), ()))
    modes = lax.dot_general(points, high, dims, preferred_element_type=jnp.float32)
    modes += lax.dot_general(points, low, dims, preferred_element_type=jnp.float32)
    modes_ref[...] = modes


def factor_call(xy, packed):
    width = packed.shape[1]
    n = width // 2
    vmem = pl.BlockSpec(memory_space=pltpu.VMEM)
    return pl.pallas_call(
        factor_kernel,
        out_shape=(
            jax.ShapeDtypeStruct((xy.shape[1], width), jnp.float32),
            jax.ShapeDtypeStruct((2, n, n), jnp.float32),
        ),
        in_specs=[vmem, vmem],
        out_specs=(vmem, vmem),
        scratch_shapes=[
            pltpu.VMEM((width, width), jnp.float32),
        ],
        name="factor_and_modes",
    )(xy, packed)


def local(space, zs, snapshots, row_scales, block_offsets, freq_index):
    xy, packed = gather_call(
        snapshots, row_scales, block_offsets, freq_index, space=space, zs=zs
    )
    xy = pltpu.with_memory_space_constraint(xy, pltpu.VMEM)
    packed = pltpu.with_memory_space_constraint(packed, pltpu.VMEM)
    modes, r_factor = factor_call(xy, packed)
    return (modes[None], r_factor[None])


def solution(mesh):
    return jax.shard_map(
        functools.partial(local, mesh.shape["space"], mesh.shape["blk"]),
        mesh=mesh,
        in_specs=(P("blk", "space"), P("blk"), P("blk"), P()),
        out_specs=(P("blk", "space", None), P("blk", None, None, None)),
        check_vma=False,
    )
```

time: 45.3 us -> 40.5 us (0.89)
  Pallas kernels: 43.1 us -> 39.7 us
  local copies, waits for them, and re-layouts: 1.29 us -> 0 us
    pallas_call x1, Pallas kernels: 36.2 us -> 33.4 us  [gather_call(): pl.pallas_call(kernel, out_shape=(pltpu.VMEM((cols, points), jnp.bfloat16...]
    broadcast_in_dim x1 -> x0, local copies, waits for them, and re-layouts: 1.29 us -> none  [local(): row_scales[None, :]]
    pallas_call x1, Pallas kernels: 6.94 us -> 6.24 us  [factor_call(): pl.pallas_call(factor_kernel, out_shape=(jax.ShapeDtypeStruct((xy.shape[1...]
where the time goes in v3:
time: 40.5 us; the launch traced here: 40.3 us
  Pallas kernels  39.7 us (98%)
  between operations  0.64 us (2%)
    pallas_call x1, Pallas kernels, gather_call(): pl.pallas_call(kernel, out_shape=(pltpu.VMEM((cols, points), jnp.bfloat16...  33.4 us
    pallas_call x1, Pallas kernels, factor_call(): pl.pallas_call(factor_kernel, out_shape=(jax.ShapeDtypeStruct((xy.shape[1...  6.24 us

profile of v3, /device:TPU:1, one launch (start us, length us, event | category | flops | bytes accessed | tf_op | source)
XLA Modules:
  0.0 40.3 jit_solution(3376342366227015167)
XLA Ops:
  0.6 33.4 %spectra_and_gram.1 = (bf16[128,512]{1,0:T(8,128)(2,1)S(1)}, f32[32,128]{1,0:T(8,128)S(1)}) custom-call(bf16[1280,512]{1,0:T(8,128)(2,1)} %snaps_hbm.1, f32[1280]{0:T(1024)} %scales_hbm.1, s32[4]{0:T(128)} %offs_hbm.1, s32[16]{0:T(128)} %freq_hbm.1), custom_call_target="tpu_custom_call" | custom-call | tf_op jit(solution)/shard_map/spectra_and_gram/pallas_call | solution.py:237
  34.1 6.2 %factor_and_modes.1 = (f32[512,128]{1,0:T(8,128)}, f32[2,64,64]{2,1,0:T(8,128)}) custom-call(bf16[128,512]{1,0:T(8,128)(2,1)S(1)} %get-tuple-element.6.xy, f32[32,128]{1,0:T(8,128)S(1)} %get-tuple-element.7.packed_ref), custom_call_target="tpu_custom_call" | custom-call | tf_op jit(solution)/shard_map/factor_and_modes/pallas_call | solution.py:370

commit v4 on v3

--- a/solution.py
+++ b/solution.py
@@ -32,7 +32,7 @@
 
 
 def sides_of(space):
-    side = {32: 4, 8: 2}[space]
+    side = {32: 4, 8: 2, 2: 1}[space]
     return side, side
 
 
@@ -94,7 +94,7 @@
     snaps_hbm, scales_hbm, offs_hbm, freq_hbm,
     xy, gram_ref,
     snaps, scales_ref, offs_ref, freq_ref, coef, table, phase, send, recv, rows32,
-    pair_buf, x_buf, y_buf,
+    x_buf, y_buf,
     load_sems, send_sems, recv_sems, gsend_sems, grecv_sems,
 ):
     ys, xs = sides
@@ -122,16 +122,20 @@
         return (yy * xs + xx) * 2 + cc
 
     z_peers = [lax.rem(z + d, zs) for d in range(1, zs)]
-    x_peers = [space_of(y, lax.rem(x + d, xs), core) for d in range(1, xs)]
-    y_peers = [space_of(lax.rem(y + d, ys), x, core) for d in range(1, ys)]
-    pair = space_of(y, x, 1 - core)
+    def far_first(n):
+        return sorted(range(1, n), key=lambda d: -min(d, n - d))
+
+    cores = (core, 1 - core)
+    x_peers = [space_of(y, lax.rem(x + d, xs), c) for d in far_first(xs) for c in cores]
+    x_peers.append(space_of(y, x, 1 - core))
+    y_peers = [space_of(lax.rem(y + d, ys), x, core) for d in far_first(ys)]
 
     barrier = pltpu.get_barrier_semaphore()
-    order = sorted(range(1, zs), key=lambda d: -min(d, zs - d))
+    order = far_first(zs)
     for d in order:
         peer = z_peers[d - 1]
         pl.semaphore_signal(barrier, inc=1, device_id={"blk": peer}, device_id_type=MESH)
-    for peer in [pair] + x_peers + y_peers:
+    for peer in x_peers + y_peers:
         pl.semaphore_signal(barrier, inc=1, device_id={"space": peer}, device_id_type=MESH)
 
     for load in loads[:3]:
@@ -147,7 +151,7 @@
         send[h] = spectra.reshape(send.shape[1:]).astype(jnp.bfloat16)
         recv[h, z] = send[h, z]
         if h == 0:
-            pl.semaphore_wait(barrier, len(z_peers) + 1 + len(x_peers) + len(y_peers))
+            pl.semaphore_wait(barrier, len(z_peers) + len(x_peers) + len(y_peers))
         for d in order:
             peer = z_peers[d - 1]
             copy = pltpu.make_async_remote_copy(
@@ -187,7 +191,7 @@
     row, lane = iota(gram.shape, 0), iota(gram.shape, 1)
     packed = jnp.where(lane >= row, gram, pltpu.roll(gram, half, 1))
     upper, lower = packed[: half // 2], pltpu.roll(packed[half // 2 :], half, 1)
-    pair_buf[core] = jnp.where(iota(upper.shape, 1) < half, upper, lower)
+    x_buf[x * 2 + core] = jnp.where(iota(upper.shape, 1) < half, upper, lower)
 
     def exchange(buf, here, peers, base):
         moves = []
@@ -212,12 +216,10 @@
             total = total + buf[i]
         return total
 
-    moves_p = exchange(pair_buf, core, [pair], 0)
-    x_buf[x] = summed(pair_buf, moves_p)
-    moves_x = exchange(x_buf, x, x_peers, 1)
+    moves_x = exchange(x_buf, x * 2 + core, x_peers, 0)
     y_buf[y] = summed(x_buf, moves_x)
-    moves_y = exchange(y_buf, y, y_peers, xs)
-    for copy in copies + moves_p + moves_x:
+    moves_y = exchange(y_buf, y, y_peers, 2 * xs)
+    for copy in copies + moves_x:
         copy.wait_send()
     gram_ref[...] = summed(y_buf, moves_y) * (1.0 / total_points)
     for move in moves_y:
@@ -253,14 +255,13 @@
             pltpu.VMEM((PARTS, zs, TILE, width), jnp.bfloat16),
             pltpu.VMEM((PARTS, zs, TILE, width), jnp.bfloat16),
             pltpu.VMEM((PARTS, width // LANES, cols, LANES), jnp.float32),
-            pltpu.VMEM((2,) + gram_shape, jnp.float32),
-            pltpu.VMEM((sides[1],) + gram_shape, jnp.float32),
+            pltpu.VMEM((2 * sides[1],) + gram_shape, jnp.float32),
             pltpu.VMEM((sides[0],) + gram_shape, jnp.float32),
             pltpu.SemaphoreType.DMA((4,)),
             pltpu.SemaphoreType.DMA((PARTS, zs)),
             pltpu.SemaphoreType.DMA((PARTS, zs)),
-            pltpu.SemaphoreType.DMA((sum(sides),)),
-            pltpu.SemaphoreType.DMA((sum(sides),)),
+            pltpu.SemaphoreType.DMA((2 * sides[1] + sides[0],)),
+            pltpu.SemaphoreType.DMA((2 * sides[1] + sides[0],)),
         ],
         compiler_params=pltpu.CompilerParams(collective_id=0, has_side_effects=True),
         name="spectra_and_gram",
@@ -269,39 +270,46 @@
 
 def unpacked(packed, n):
     both = jnp.concatenate([packed, pltpu.roll(packed, n, 1)], 0)
-    flipped = both.T
-    flipped = flipped[:n, :]
+    flipped = both.T[:n, :]
     row, lane = iota((n, n), 0), iota((n, n), 1)
     both = both[:, :n]
     real = jnp.where(lane >= row, both, flipped)
     imag = jnp.where(lane < row, both, jnp.where(lane > row, -flipped, 0.0))
-    return jnp.concatenate([real, imag], 1)
+    return real, imag
+
+
+def in_three(value):
+    high = value.astype(jnp.bfloat16)
+    rest = value - high.astype(jnp.float32)
+    middle = rest.astype(jnp.bfloat16)
+    low = (rest - middle.astype(jnp.float32)).astype(jnp.bfloat16)
+    return high, middle, low
 
 
 def factor_kernel(xy, packed_ref, modes_ref, r_ref, w_ref):
     width = packed_ref.shape[1]
     n = width // 2
     tiles = n // TILE
-    gram = unpacked(packed_ref[...], n)
+    real, imag = unpacked(packed_ref[...], n)
     lane, sub = iota((TILE, width), 1), iota((TILE, width), 0)
-    sign = jnp.where(lane < n, -1.0, 1.0)
-
-    def turn(value):
-        return pltpu.roll(value, n, 1) * sign
 
     def spread(value, row):
-        return jnp.broadcast_to(value[row : row + 1, :], (TILE, width))
+        return jnp.take_along_axis(value, jnp.full((TILE, width), row, jnp.int32), 0, mode="promise_in_bounds")
 
     def across(value, column):
         return jnp.broadcast_to(value[:, column : column + 1], (TILE, width))
 
-    cs = [gram[TILE * i : TILE * (i + 1), :] for i in range(tiles)]
-    ls = [jnp.where(lane == sub + TILE * i, 1.0, 0.0) for i in range(tiles)]
+    ps, qs = [], []
+    for i in range(tiles):
+        rows = slice(TILE * i, TILE * (i + 1))
+        unit = jnp.where(iota((TILE, n), 1) == iota((TILE, n), 0) + TILE * i, 1.0, 0.0)
+        ps.append(jnp.concatenate([real[rows], unit], 1))
+        qs.append(jnp.concatenate([imag[rows], jnp.zeros((TILE, n), jnp.float32)], 1))
 
     for panel in range(tiles):
         group = [panel] + ([panel + 1] if panel + 1 < tiles else [])
-        res = {i: [across(cs[i], TILE * panel + j) for j in range(TILE)] for i in group}
-        ims = {i: [across(cs[i], n + TILE * panel + j) for j in range(TILE)] for i in group}
+        res = {i: [across(ps[i], TILE * panel + j) for j in range(TILE)] for i in group}
+        ims = {i: [across(qs[i], TILE * panel + j) for j in range(TILE)] for i in group}
         scale = jnp.zeros((TILE, width), jnp.float32)
         for k in range(TILE):
             pivot = spread(res[panel][k], k)
@@ -314,44 +322,40 @@
                     mr, mi = mults[i]
                     res[i][j] = res[i][j] - (mr * pr - mi * pi)
                     ims[i][j] = ims[i][j] - (mr * pi + mi * pr)
-            c_row, l_row = spread(cs[panel], k), spread(ls[panel], k)
-            c_turn, l_turn = turn(c_row), turn(l_row)
+            p_row, q_row = spread(ps[panel], k), spread(qs[panel], k)
             for i in group:
                 mr, mi = mults[i]
                 if i == panel:
                     mr, mi = jnp.where(sub > k, mr, 0.0), jnp.where(sub > k, mi, 0.0)
-                cs[i] = cs[i] - (mr * c_row + mi * c_turn)
-                ls[i] = ls[i] - (mr * l_row + mi * l_turn)
-        r_rows = cs[panel] * scale
-        l_rows = ls[panel] * scale
+                ps[i] = ps[i] - (mr * p_row - mi * q_row)
+                qs[i] = qs[i] - (mr * q_row + mi * p_row)
+        p_rows = ps[panel] * scale
+        q_rows = qs[panel] * scale
         if panel + 2 < tiles:
-            first = TILE * (panel + 2)
-            lhs = jnp.concatenate([r_rows, pltpu.roll(r_rows, n, 1)], 0)
-            rhs = jnp.concatenate(
-                [
-                    jnp.concatenate([r_rows, l_rows], 1),
-                    jnp.concatenate([-turn(r_rows), -turn(l_rows)], 1),
-                ],
-                0,
-            )
+            parts_p, parts_q = in_three(p_rows), in_three(q_rows)
+            lhs, rhs = [], []
+            for i, j in ((0, 0), (0, 1), (1, 0), (0, 2), (2, 0), (1, 1)):
+                lhs += [parts_p[i], parts_q[i]]
+                rhs.append(jnp.concatenate([parts_p[j], parts_q[j]], 1))
+                rhs.append(jnp.concatenate([parts_q[j], -parts_p[j]], 1))
             update = lax.dot_general(
-                lhs[:, :n],
-                rhs,
+                jnp.concatenate(lhs, 0)[:, :n],
+                jnp.concatenate(rhs, 0),
                 (((0,), (0,)), ((), ())),
-                precision=lax.Precision.HIGHEST,
                 preferred_element_type=jnp.float32,
             )
             for i in range(panel + 2, tiles):
                 part = update[TILE * i : TILE * (i + 1), :]
-                cs[i] = cs[i] - part[:, :width]
-                ls[i] = ls[i] - part[:, width:]
+                ps[i] = ps[i] - part[:, :width]
+                qs[i] = qs[i] - part[:, width:]
         row = sub + TILE * panel
-        keep = (lane >= row) & ((lane < n) | (lane - n > row))
-        r_rows = jnp.where(keep, r_rows, 0.0)
-        r_ref[0, pl.ds(TILE * panel, TILE), :] = r_rows[:, :n]
-        r_ref[1, pl.ds(TILE * panel, TILE), :] = pltpu.roll(r_rows, n, 1)[:, :n]
-        w_ref[pl.ds(2 * TILE * panel, TILE, stride=2), :] = l_rows
-        w_ref[pl.ds(2 * TILE * panel + 1, TILE, stride=2), :] = turn(l_rows)
+        here = pl.ds(TILE * panel, TILE)
+        r_ref[0, here, :] = jnp.where(lane >= row, p_rows, 0.0)[:, :n]
+        r_ref[1, here, :] = jnp.where(lane > row, q_rows, 0.0)[:, :n]
+        even = jnp.where(lane < n, pltpu.roll(p_rows, n, 1), q_rows)
+        odd = jnp.where(lane < n, -pltpu.roll(q_rows, n, 1), p_rows)
+        w_ref[pl.ds(2 * TILE * panel, TILE, stride=2), :] = even
+        w_ref[pl.ds(2 * TILE * panel + 1, TILE, stride=2), :] = odd
 
     w = w_ref[...]
     high = w.astype(jnp.bfloat16)

time: 40.5 us -> 36.8 us (0.909)
  Pallas kernels: 39.7 us -> 36 us
    pallas_call x1, Pallas kernels: 6.24 us -> 3.02 us  [factor_call(): pl.pallas_call(factor_kernel, out_shape=(jax.ShapeDtypeStruct((xy.shape[1...]
    pallas_call x1, Pallas kernels: 33.4 us -> 33 us  [gather_call(): pl.pallas_call(kernel, out_shape=(pltpu.VMEM((cols, points), jnp.bfloat16...]
where the time goes in v4:
time: 36.8 us; the launch traced here: 36.6 us
  Pallas kernels  36 us (98%)
  between operations  0.64 us (2%)
    pallas_call x1, Pallas kernels, gather_call(): pl.pallas_call(kernel, out_shape=(pltpu.VMEM((cols, points), jnp.bfloat16...  33 us
    pallas_call x1, Pallas kernels, factor_call(): pl.pallas_call(factor_kernel, out_shape=(jax.ShapeDtypeStruct((xy.shape[1...  3.02 us

profile of v4, /device:TPU:1, one launch (start us, length us, event | category | flops | bytes accessed | tf_op | source)
XLA Modules:
  0.0 36.6 jit_solution(18234134902833747650)
XLA Ops:
  0.6 33.0 %spectra_and_gram.1 = (bf16[128,512]{1,0:T(8,128)(2,1)S(1)}, f32[32,128]{1,0:T(8,128)S(1)}) custom-call(bf16[1280,512]{1,0:T(8,128)(2,1)} %snaps_hbm.1, f32[1280]{0:T(1024)} %scales_hbm.1, s32[4]{0:T(128)} %offs_hbm.1, s32[16]{0:T(128)} %freq_hbm.1), custom_call_target="tpu_custom_call" | custom-call | tf_op jit(solution)/shard_map/spectra_and_gram/pallas_call | solution.py:239
  33.6 3.0 %factor_and_modes.1 = (f32[512,128]{1,0:T(8,128)}, f32[2,64,64]{2,1,0:T(8,128)}) custom-call(bf16[128,512]{1,0:T(8,128)(2,1)S(1)} %get-tuple-element.6.xy, f32[32,128]{1,0:T(8,128)S(1)} %get-tuple-element.7.packed_ref), custom_call_target="tpu_custom_call" | custom-call | tf_op jit(solution)/shard_map/factor_and_modes/pallas_call | solution.py:374

commit v5 on v4

--- a/solution.py
+++ b/solution.py
@@ -100,9 +100,17 @@
     ys, xs = sides
     z = lax.axis_index("blk")
     s = lax.axis_index("space")
-    core = lax.rem(s, 2)
-    x = lax.rem(s // 2, xs)
-    y = s // (2 * xs)
+
+    z_peers = [lax.rem(z + d, zs) for d in range(1, zs)]
+
+    def far_first(n):
+        return sorted(range(1, n), key=lambda d: -min(d, n - d))
+
+    barrier = pltpu.get_barrier_semaphore()
+    order = far_first(zs)
+    for d in order:
+        peer = z_peers[d - 1]
+        pl.semaphore_signal(barrier, inc=1, device_id={"blk": peer}, device_id_type=MESH)
 
     loads = [
         pltpu.make_async_copy(source, target, load_sems.at[i])
@@ -118,23 +126,18 @@
     for load in loads:
         load.start()
 
+    core = lax.rem(s, 2)
+    x = lax.rem(s // 2, xs)
+    y = s // (2 * xs)
+
     def space_of(yy, xx, cc):
         return (yy * xs + xx) * 2 + cc
-
-    z_peers = [lax.rem(z + d, zs) for d in range(1, zs)]
-    def far_first(n):
-        return sorted(range(1, n), key=lambda d: -min(d, n - d))
 
     cores = (core, 1 - core)
     x_peers = [space_of(y, lax.rem(x + d, xs), c) for d in far_first(xs) for c in cores]
     x_peers.append(space_of(y, x, 1 - core))
     y_peers = [space_of(lax.rem(y + d, ys), x, core) for d in far_first(ys)]
 
-    barrier = pltpu.get_barrier_semaphore()
-    order = far_first(zs)
-    for d in order:
-        peer = z_peers[d - 1]
-        pl.semaphore_signal(barrier, inc=1, device_id={"blk": peer}, device_id_type=MESH)
     for peer in x_peers + y_peers:
         pl.semaphore_signal(barrier, inc=1, device_id={"space": peer}, device_id_type=MESH)
 

time: 36.8 us -> 36.7 us (level)
  no operation moved by 1% of the time
where the time goes in v5:
time: 36.7 us; the launch traced here: 36.6 us
  Pallas kernels  36 us (98%)
  between operations  0.64 us (2%)
    pallas_call x1, Pallas kernels, gather_call(): pl.pallas_call(kernel, out_shape=(pltpu.VMEM((cols, points), jnp.bfloat16...  32.9 us
    pallas_call x1, Pallas kernels, factor_call(): pl.pallas_call(factor_kernel, out_shape=(jax.ShapeDtypeStruct((xy.shape[1...  3.02 us

profile of v5, /device:TPU:1, one launch (start us, length us, event | category | flops | bytes accessed | tf_op | source)
XLA Modules:
  0.0 36.6 jit_solution(16042393660759419736)
XLA Ops:
  0.6 32.9 %spectra_and_gram.1 = (bf16[128,512]{1,0:T(8,128)(2,1)S(1)}, f32[32,128]{1,0:T(8,128)S(1)}) custom-call(bf16[1280,512]{1,0:T(8,128)(2,1)} %snaps_hbm.1, f32[1280]{0:T(1024)} %scales_hbm.1, s32[4]{0:T(128)} %offs_hbm.1, s32[16]{0:T(128)} %freq_hbm.1), custom_call_target="tpu_custom_call" | custom-call | tf_op jit(solution)/shard_map/spectra_and_gram/pallas_call | solution.py:242
  33.6 3.0 %factor_and_modes.1 = (f32[512,128]{1,0:T(8,128)}, f32[2,64,64]{2,1,0:T(8,128)}) custom-call(bf16[128,512]{1,0:T(8,128)(2,1)S(1)} %get-tuple-element.6.xy, f32[32,128]{1,0:T(8,128)S(1)} %get-tuple-element.7.packed_ref), custom_call_target="tpu_custom_call" | custom-call | tf_op jit(solution)/shard_map/factor_and_modes/pallas_call | solution.py:377
